TPU v7x, 256 devices: a whole 4x4x8 slice. The times are simulated.
256 devices in a mesh: row: 8 (over x, core), col: 32 (over y, z).
Axes of the slice: x: 4, y: 4, z: 8, core: 2. Of those that a mesh axis runs over, the one named last changes fastest.
Arguments:
- upper_panel: float32 [2048, 8192], P('row', 'col')
- lower_panel: float32 [2048, 8192], P('row', 'col')
- pole_values: float32 [2, 8192], P(None, 'col'), may hold values from 0 to 4, as said below
- coupling: float32 [2, 8192], P(None, 'col'), may hold values from -6 to 6
- kept_mask: int32 [2, 8192], P(None, 'col'), may hold values from 0 to 1, as said below
- shifts: float32 [16384], P('col'), may hold values from 0 to 4
- source: int32 [16384], P('col'), may hold values from 0 to 16384, as said below
Outputs:
- vectors: float32 [2, 2048, 16384], P(None, 'row', 'col')
- slab_weight: float32 [16384], P('col')
Inputs may be any that keep to these rules, and one draw needn't show every extreme that they name: source[j] = 16384 marks an undeflated merged column; any other value is the pole whose child column the merged column copies, and no pole is named twice. Each device's 512 merged columns hold from 64 to 384 undeflated columns, and some device holds exactly 384. kept_mask is 0 exactly at the poles named in source. Some device of col holds no deflated pole: every pole of both children that it holds is kept. `pole_values`: every pole lies at least 0.4 / 16384 away from every entry of shifts.
All inputs are finite; a program needn't handle non-finite values.
Results may differ from a plain program's by a relative error of at most 0.0003.
Values sent between devices are 32-bit elements; how exact they have to be, the bound alone decides.
A program may use at most 64 MiB of HBM per device.

v0:
```python
import math
import jax
import jax.numpy as jnp
from jax import lax
from jax.sharding import PartitionSpec as P

N1 = 8192
exact_mode = lax.Precision.HIGHEST


def cauchy_block(pole_vals, weights, shift_vals):
    return weights[:, :, None] / (pole_vals[:, :, None] - shift_vals[None, None, :])


def local(upper_panel, lower_panel, pole_values, coupling, kept_mask, shifts, source):
    rows_here = upper_panel.shape[0]
    own_cols = shifts.shape[0]
    weighted = coupling * kept_mask.astype(jnp.float32)
    undeflated = source == 2 * N1
    child_base = jnp.array([0, N1], jnp.int32)
    zeros_acc = jnp.zeros((rows_here, own_cols), jnp.float32)
    pieces = (
        lax.all_gather(upper_panel, "col", axis=1, tiled=True),
        lax.all_gather(lower_panel, "col", axis=1, tiled=True),
        lax.all_gather(pole_values, "col", axis=1, tiled=True),
        lax.all_gather(weighted, "col", axis=1, tiled=True),
    )
    span_cols = math.gcd(pieces[0].shape[1], 1024)

    def advance(number, running):
        window = [
            lax.dynamic_slice_in_dim(member, number * span_cols, span_cols, 1) for member in pieces
        ]
        first_pole = number * span_cols
        cauchy = cauchy_block(window[2], window[3], shifts)
        indices = first_pole + lax.iota(jnp.int32, span_cols)
        one_hot = indices[None, :, None] + child_base[:, None, None] == source[None, None, :]
        basis_tile = jnp.where(undeflated[None, None, :], cauchy, one_hot.astype(jnp.float32))
        upper_acc = running[0] + jnp.dot(
            window[0], basis_tile[0], precision=exact_mode, preferred_element_type=jnp.float32
        )
        lower_acc = running[1] + jnp.dot(
            window[1], basis_tile[1], precision=exact_mode, preferred_element_type=jnp.float32
        )
        return (upper_acc, lower_acc, running[2] + jnp.sum(cauchy * cauchy, axis=(0, 1)))

    upper_acc, lower_acc, norm_sums = lax.fori_loop(
        0,
        pieces[0].shape[1] // span_cols,
        advance,
        (zeros_acc, zeros_acc, jnp.zeros((own_cols,), jnp.float32)),
    )
    scaling = jnp.where(undeflated, lax.rsqrt(norm_sums), 1.0)
    vectors = jnp.stack([upper_acc * scaling[None, :], lower_acc * scaling[None, :]])
    partial_weight = jnp.sum(vectors * vectors, axis=(0, 1))
    slab_weight = lax.psum(partial_weight, "row") / (2 * rows_here * lax.axis_size("row"))
    return (vectors, slab_weight)


def solution(mesh):
    in_specs = (
        P("row", "col"),
        P("row", "col"),
        P(None, "col"),
        P(None, "col"),
        P(None, "col"),
        P("col"),
        P("col"),
    )
    out_specs = (P(None, "row", "col"), P("col"))
    return jax.shard_map(local, mesh=mesh, in_specs=in_specs, out_specs=out_specs, check_vma=False)
```

profile of v0, /device:TPU:1, one launch (start us, length us, event | category | flops | bytes accessed | tf_op | source)
XLA Modules:
  0.0 310.2 jit_solution(16482954497444541827)
XLA Ops:
  7.2 0.0 all-gather.3.cloned.1.call-start
  7.2 0.7 all-gather.3.cloned.1.call-update
  7.9 0.0 all-gather.5.cloned.1.call-start
  7.9 0.7 all-gather.5.cloned.1.call-update
  8.7 0.7 convert_multiply_fusion
  9.4 41.5 %all_gather.13 = f32[2,8192]{1,0:T(2,128)S(1)} all-gather(f32[2,256]{1,0:T(2,128)S(1)} %convert_multiply_fusion), channel_id=1, replica_groups=mesh['row'=8,'col'=32] {'col'}, dimensions={1}, use_global_device_ids=true | all-gather | bytes 67584 | tf_op jit(solution)/shard_map/all_gather | solution.py:26
  50.9 39.2 %all_gather.14 = f32[2,8192]{1,0:T(2,128)S(1)} all-gather(f32[2,256]{1,0:T(2,128)} %param.12), channel_id=1, replica_groups=mesh['row'=8,'col'=32] {'col'}, dimensions={1}, use_global_device_ids=true | all-gather | bytes 67584 | tf_op jit(solution)/shard_map/all_gather | solution.py:25
  90.1 0.7 broadcast_compare_fusion
  90.8 23.1 %all-gather.3.cloned.1.call-done = f32[256,8192]{1,0:T(8,128)} async-done(((f32[256,256]{1,0:T(8,128)}), f32[256,8192]{1,0:T(8,128)}) %all-gather.3.cloned.1.call-update) | async-done | bytes 8388624 | tf_op jit(solution)/shard_map/all_gather | solution.py:23
  113.9 102.9 %all-gather.5.cloned.1.call-done = f32[256,8192]{1,0:T(8,128)} async-done(((f32[256,256]{1,0:T(8,128)}), f32[256,8192]{1,0:T(8,128)}) %all-gather.5.cloned.1.call-update) | async-done | bytes 8388624 | tf_op jit(solution)/shard_map/all_gather | solution.py:24
  216.8 68.3 %while.18 = (s32[]{:T(128)}, f32[256,512]{1,0:T(8,128)S(1)}, f32[256,512]{1,0:T(8,128)S(1)}, f32[512]{0:T(512)S(1)}, f32[256,8192]{1,0:T(8,128)}, /*index=5*/pre...) while((s32[]{:T(128)}, f32[256,512]{1,0:T(8,128)S(1)}, ...), condition=%wide.region_2.3_spmd.clone, body=%wide.region_0.2_spmd.clone.sunk | while | flops 3229093376 | bytes 12669679 | solution.py:47
  216.9 0.1 broadcast_add_fusion.2
  216.9 1.9 multiply_reduce_fusion.3
  218.8 3.3 %fusion.17 = f32[256,512]{1,0:T(8,128)S(1)} fusion(f32[2,1024,512]{2,1,0:T(8,128)S(1)} %get-tuple-element.347, f32[256,8192]{1,0:T(8,128)} %get-tuple-element.389, s32[]{:T(128)S(6)} %select_n.28, f32[256,512]{1,0:T(8,128)S(1)} %get-tuple-element.366, pred[]{:T(512)S(6)} %compare.3), kind=kOutput, calls=%fused_computation.9.clone.1 | convolution fusion | flops 1610874880 | bytes 4194309 | tf_op jit(solution)/shard_map/while/body/eval_jaxpr/dot_general | solution.py:42
  222.1 3.3 %fusion.16 = f32[256,512]{1,0:T(8,128)S(1)} fusion(f32[2,1024,512]{2,1,0:T(8,128)S(1)} %get-tuple-element.347, f32[256,8192]{1,0:T(8,128)} %get-tuple-element.383, s32[]{:T(128)S(6)} %select_n.28, f32[256,512]{1,0:T(8,128)S(1)} %get-tuple-element.365, pred[]{:T(512)S(6)} %compare.3), kind=kOutput, calls=%fused_computation.8.clone.1 | convolution fusion | flops 1610874880 | bytes 4194309 | tf_op jit(solution)/shard_map/while/body/eval_jaxpr/dot_general | solution.py:39
  225.4 0.1 broadcast_add_fusion.2
  225.5 1.9 multiply_reduce_fusion.3
  227.4 3.3 %fusion.17 = f32[256,512]{1,0:T(8,128)S(1)} fusion(f32[2,1024,512]{2,1,0:T(8,128)S(1)} %get-tuple-element.347, f32[256,8192]{1,0:T(8,128)} %get-tuple-element.389, s32[]{:T(128)S(6)} %select_n.28, f32[256,512]{1,0:T(8,128)S(1)} %get-tuple-element.366, pred[]{:T(512)S(6)} %compare.3), kind=kOutput, calls=%fused_computation.9.clone.1 | convolution fusion | flops 1610874880 | bytes 4194309 | tf_op jit(solution)/shard_map/while/body/eval_jaxpr/dot_general | solution.py:42
  230.6 3.3 %fusion.16 = f32[256,512]{1,0:T(8,128)S(1)} fusion(f32[2,1024,512]{2,1,0:T(8,128)S(1)} %get-tuple-element.347, f32[256,8192]{1,0:T(8,128)} %get-tuple-element.383, s32[]{:T(128)S(6)} %select_n.28, f32[256,512]{1,0:T(8,128)S(1)} %get-tuple-element.365, pred[]{:T(512)S(6)} %compare.3), kind=kOutput, calls=%fused_computation.8.clone.1 | convolution fusion | flops 1610874880 | bytes 4194309 | tf_op jit(solution)/shard_map/while/body/eval_jaxpr/dot_general | solution.py:39
  233.9 0.1 broadcast_add_fusion.2
  234.0 1.9 multiply_reduce_fusion.3
  235.9 3.3 %fusion.17 = f32[256,512]{1,0:T(8,128)S(1)} fusion(f32[2,1024,512]{2,1,0:T(8,128)S(1)} %get-tuple-element.347, f32[256,8192]{1,0:T(8,128)} %get-tuple-element.389, s32[]{:T(128)S(6)} %select_n.28, f32[256,512]{1,0:T(8,128)S(1)} %get-tuple-element.366, pred[]{:T(512)S(6)} %compare.3), kind=kOutput, calls=%fused_computation.9.clone.1 | convolution fusion | flops 1610874880 | bytes 4194309 | tf_op jit(solution)/shard_map/while/body/eval_jaxpr/dot_general | solution.py:42
  239.2 3.3 %fusion.16 = f32[256,512]{1,0:T(8,128)S(1)} fusion(f32[2,1024,512]{2,1,0:T(8,128)S(1)} %get-tuple-element.347, f32[256,8192]{1,0:T(8,128)} %get-tuple-element.383, s32[]{:T(128)S(6)} %select_n.28, f32[256,512]{1,0:T(8,128)S(1)} %get-tuple-element.365, pred[]{:T(512)S(6)} %compare.3), kind=kOutput, calls=%fused_computation.8.clone.1 | convolution fusion | flops 1610874880 | bytes 4194309 | tf_op jit(solution)/shard_map/while/body/eval_jaxpr/dot_general | solution.py:39
  242.5 0.1 broadcast_add_fusion.2
  242.6 1.9 multiply_reduce_fusion.3
  244.5 3.3 %fusion.17 = f32[256,512]{1,0:T(8,128)S(1)} fusion(f32[2,1024,512]{2,1,0:T(8,128)S(1)} %get-tuple-element.347, f32[256,8192]{1,0:T(8,128)} %get-tuple-element.389, s32[]{:T(128)S(6)} %select_n.28, f32[256,512]{1,0:T(8,128)S(1)} %get-tuple-element.366, pred[]{:T(512)S(6)} %compare.3), kind=kOutput, calls=%fused_computation.9.clone.1 | convolution fusion | flops 1610874880 | bytes 4194309 | tf_op jit(solution)/shard_map/while/body/eval_jaxpr/dot_general | solution.py:42
  247.7 3.3 %fusion.16 = f32[256,512]{1,0:T(8,128)S(1)} fusion(f32[2,1024,512]{2,1,0:T(8,128)S(1)} %get-tuple-element.347, f32[256,8192]{1,0:T(8,128)} %get-tuple-element.383, s32[]{:T(128)S(6)} %select_n.28, f32[256,512]{1,0:T(8,128)S(1)} %get-tuple-element.365, pred[]{:T(512)S(6)} %compare.3), kind=kOutput, calls=%fused_computation.8.clone.1 | convolution fusion | flops 1610874880 | bytes 4194309 | tf_op jit(solution)/shard_map/while/body/eval_jaxpr/dot_general | solution.py:39
  251.0 0.1 broadcast_add_fusion.2
  251.1 1.9 multiply_reduce_fusion.3
  253.0 3.3 %fusion.17 = f32[256,512]{1,0:T(8,128)S(1)} fusion(f32[2,1024,512]{2,1,0:T(8,128)S(1)} %get-tuple-element.347, f32[256,8192]{1,0:T(8,128)} %get-tuple-element.389, s32[]{:T(128)S(6)} %select_n.28, f32[256,512]{1,0:T(8,128)S(1)} %get-tuple-element.366, pred[]{:T(512)S(6)} %compare.3), kind=kOutput, calls=%fused_computation.9.clone.1 | convolution fusion | flops 1610874880 | bytes 4194309 | tf_op jit(solution)/shard_map/while/body/eval_jaxpr/dot_general | solution.py:42
  256.3 3.3 %fusion.16 = f32[256,512]{1,0:T(8,128)S(1)} fusion(f32[2,1024,512]{2,1,0:T(8,128)S(1)} %get-tuple-element.347, f32[256,8192]{1,0:T(8,128)} %get-tuple-element.383, s32[]{:T(128)S(6)} %select_n.28, f32[256,512]{1,0:T(8,128)S(1)} %get-tuple-element.365, pred[]{:T(512)S(6)} %compare.3), kind=kOutput, calls=%fused_computation.8.clone.1 | convolution fusion | flops 1610874880 | bytes 4194309 | tf_op jit(solution)/shard_map/while/body/eval_jaxpr/dot_general | solution.py:39
  259.6 0.1 broadcast_add_fusion.2
  259.6 1.9 multiply_reduce_fusion.3
  261.5 3.3 %fusion.17 = f32[256,512]{1,0:T(8,128)S(1)} fusion(f32[2,1024,512]{2,1,0:T(8,128)S(1)} %get-tuple-element.347, f32[256,8192]{1,0:T(8,128)} %get-tuple-element.389, s32[]{:T(128)S(6)} %select_n.28, f32[256,512]{1,0:T(8,128)S(1)} %get-tuple-element.366, pred[]{:T(512)S(6)} %compare.3), kind=kOutput, calls=%fused_computation.9.clone.1 | convolution fusion | flops 1610874880 | bytes 4194309 | tf_op jit(solution)/shard_map/while/body/eval_jaxpr/dot_general | solution.py:42
  264.8 3.3 %fusion.16 = f32[256,512]{1,0:T(8,128)S(1)} fusion(f32[2,1024,512]{2,1,0:T(8,128)S(1)} %get-tuple-element.347, f32[256,8192]{1,0:T(8,128)} %get-tuple-element.383, s32[]{:T(128)S(6)} %select_n.28, f32[256,512]{1,0:T(8,128)S(1)} %get-tuple-element.365, pred[]{:T(512)S(6)} %compare.3), kind=kOutput, calls=%fused_computation.8.clone.1 | convolution fusion | flops 1610874880 | bytes 4194309 | tf_op jit(solution)/shard_map/while/body/eval_jaxpr/dot_general | solution.py:39
  268.1 0.1 broadcast_add_fusion.2
  268.2 1.9 multiply_reduce_fusion.3
  270.1 3.3 %fusion.17 = f32[256,512]{1,0:T(8,128)S(1)} fusion(f32[2,1024,512]{2,1,0:T(8,128)S(1)} %get-tuple-element.347, f32[256,8192]{1,0:T(8,128)} %get-tuple-element.389, s32[]{:T(128)S(6)} %select_n.28, f32[256,512]{1,0:T(8,128)S(1)} %get-tuple-element.366, pred[]{:T(512)S(6)} %compare.3), kind=kOutput, calls=%fused_computation.9.clone.1 | convolution fusion | flops 1610874880 | bytes 4194309 | tf_op jit(solution)/shard_map/while/body/eval_jaxpr/dot_general | solution.py:42
  273.3 3.3 %fusion.16 = f32[256,512]{1,0:T(8,128)S(1)} fusion(f32[2,1024,512]{2,1,0:T(8,128)S(1)} %get-tuple-element.347, f32[256,8192]{1,0:T(8,128)} %get-tuple-element.383, s32[]{:T(128)S(6)} %select_n.28, f32[256,512]{1,0:T(8,128)S(1)} %get-tuple-element.365, pred[]{:T(512)S(6)} %compare.3), kind=kOutput, calls=%fused_computation.8.clone.1 | convolution fusion | flops 1610874880 | bytes 4194309 | tf_op jit(solution)/shard_map/while/body/eval_jaxpr/dot_general | solution.py:39
  276.6 0.1 broadcast_add_fusion.2
  276.7 1.9 multiply_reduce_fusion.3
  278.6 3.3 %fusion.17 = f32[256,512]{1,0:T(8,128)S(1)} fusion(f32[2,1024,512]{2,1,0:T(8,128)S(1)} %get-tuple-element.347, f32[256,8192]{1,0:T(8,128)} %get-tuple-element.389, s32[]{:T(128)S(6)} %select_n.28, f32[256,512]{1,0:T(8,128)S(1)} %get-tuple-element.366, pred[]{:T(512)S(6)} %compare.3), kind=kOutput, calls=%fused_computation.9.clone.1 | convolution fusion | flops 1610874880 | bytes 4194309 | tf_op jit(solution)/shard_map/while/body/eval_jaxpr/dot_general | solution.py:42
  281.9 3.3 %fusion.16 = f32[256,512]{1,0:T(8,128)S(1)} fusion(f32[2,1024,512]{2,1,0:T(8,128)S(1)} %get-tuple-element.347, f32[256,8192]{1,0:T(8,128)} %get-tuple-element.383, s32[]{:T(128)S(6)} %select_n.28, f32[256,512]{1,0:T(8,128)S(1)} %get-tuple-element.365, pred[]{:T(512)S(6)} %compare.3), kind=kOutput, calls=%fused_computation.8.clone.1 | convolution fusion | flops 1610874880 | bytes 4194309 | tf_op jit(solution)/shard_map/while/body/eval_jaxpr/dot_general | solution.py:39
  285.2 0.7 rsqrt_select_fusion
  285.8 0.1 multiply_bitcast_fusion.1
  286.0 1.1 multiply_reduce_fusion.1
  287.1 15.6 %psum.7 = f32[512]{0:T(512)S(1)} all-reduce(f32[512]{0:T(512)S(1)} %get-tuple-element.266), channel_id=1, replica_groups=mesh['row'=8,'col'=32] {'row'}, use_global_device_ids=true, to_apply=%region_4.5 | all-reduce | flops 512 | bytes 4096 | tf_op jit(solution)/shard_map/psum | solution.py:56
  302.7 0.6 broadcast_multiply_fusion
  (35 shorter events, 0.2 us)
Async XLA Ops:
  7.2 106.8 %all-gather.3.cloned.1.call-start = ((), (), s32[]{:S(2)}) async-start(), calls=%async_computation | async-start | bytes 8650752 | tf_op jit(solution)/shard_map/all_gather | solution.py:23
  7.9 209.0 %all-gather.5.cloned.1.call-start = ((), (), s32[]{:S(2)}) async-start(), calls=%async_computation.1 | async-start | bytes 8650752 | tf_op jit(solution)/shard_map/all_gather | solution.py:24
Sparse Core Ops, SparseCore 0:
  10.4 103.4 all-gather.2
  116.4 100.4 all-gather.4
where the time goes:
time: 311 us; the launch traced here: 310 us
  waiting for transfers between devices  127 us (41%)
  blocking collectives  96.3 us (31%)
  matrix products  52.1 us (17%)
  other arithmetic  19.7 us (6%)
  between operations  14.1 us (5%)
    all_gather x1, waiting for transfers between devices, local(): lax.all_gather(lower_panel, 'col', axis=1, tiled=True)  103 us
    all_gather x1, blocking collectives, local(): lax.all_gather(weighted, 'col', axis=1, tiled=True)  41.5 us
    all_gather x1, blocking collectives, local(): lax.all_gather(pole_values, 'col', axis=1, tiled=True)  39.2 us
    dot_general x8, matrix products, advance(): jnp.dot(window[0], basis_tile[0], precision=exact_mode, preferred_element...  26 us
    dot_general x8, matrix products, advance(): jnp.dot(window[1], basis_tile[1], precision=exact_mode, preferred_element...  26 us
    all_gather x1, waiting for transfers between devices, local(): lax.all_gather(upper_panel, 'col', axis=1, tiled=True)  23.1 us
    psum x1, blocking collectives, local(): lax.psum(partial_weight, 'row') / (2 * rows_here * lax.axis_size('row'))  15.6 us
    reduce_sum x8, other arithmetic, advance(): jnp.sum(cauchy * cauchy, axis=(0, 1))  15 us
  transfers between devices with their start and end apart: 2, of which 2 were waited for; matrix products, arithmetic and copies ran while one was open for 0% of the time, Pallas kernels for 0%

commit v1 on v0

--- a/solution.py
+++ b/solution.py
@@ -3,6 +3,7 @@
 import jax.numpy as jnp
 from jax import lax
 from jax.sharding import PartitionSpec as P
+from jax.lax import all_gather
 
 N1 = 8192
 exact_mode = lax.Precision.HIGHEST
@@ -23,7 +24,7 @@
         lax.all_gather(upper_panel, "col", axis=1, tiled=True),
         lax.all_gather(lower_panel, "col", axis=1, tiled=True),
         lax.all_gather(pole_values, "col", axis=1, tiled=True),
-        lax.all_gather(weighted, "col", axis=1, tiled=True),
+        jnp.concatenate(all_gather(weighted, "col"), axis=1),
     )
     span_cols = math.gcd(pieces[0].shape[1], 1024)
 

time: 311 us -> 311 us (level)
  no operation moved by 1% of the time
where the time goes in v1:
time: 311 us; the launch traced here: 310 us
  waiting for transfers between devices  127 us (41%)
  blocking collectives  96.3 us (31%)
  matrix products  52.1 us (17%)
  other arithmetic  19.7 us (6%)
  between operations  14.1 us (5%)
    all_gather x1, waiting for transfers between devices, local(): lax.all_gather(lower_panel, 'col', axis=1, tiled=True)  103 us
    all_gather x1, blocking collectives, local(): all_gather(weighted, 'col')  41.5 us
    all_gather x1, blocking collectives, local(): lax.all_gather(pole_values, 'col', axis=1, tiled=True)  39.2 us
    dot_general x8, matrix products, advance(): jnp.dot(window[0], basis_tile[0], precision=exact_mode, preferred_element...  26 us
    dot_general x8, matrix products, advance(): jnp.dot(window[1], basis_tile[1], precision=exact_mode, preferred_element...  26 us
    all_gather x1, waiting for transfers between devices, local(): lax.all_gather(upper_panel, 'col', axis=1, tiled=True)  23.1 us
    psum x1, blocking collectives, local(): lax.psum(partial_weight, 'row') / (2 * rows_here * lax.axis_size('row'))  15.6 us
    reduce_sum x8, other arithmetic, advance(): jnp.sum(cauchy * cauchy, axis=(0, 1))  15 us
  transfers between devices with their start and end apart: 2, of which 2 were waited for; matrix products, arithmetic and copies ran while one was open for 0% of the time, Pallas kernels for 0%

profile of v1, /device:TPU:1, one launch (start us, length us, event | category | flops | bytes accessed | tf_op | source)
XLA Modules:
  0.0 310.2 jit_solution(17021202918650420559)
XLA Ops:
  7.2 0.0 all-gather.5.cloned.1.call-start
  7.2 0.7 all-gather.5.cloned.1.call-update
  7.9 0.0 all-gather.7.cloned.1.call-start
  7.9 0.7 all-gather.7.cloned.1.call-update
  8.7 0.7 multiply_bitcast_fusion.2
  9.4 41.5 %all-gather.1 = f32[32,2,256]{2,1,0:T(2,128)S(1)} all-gather(f32[1,2,256]{2,1,0:T(2,128)S(1)} %multiply_bitcast_fusion.2), channel_id=2, replica_groups=mesh['row'=8,'col'=32] {'col'}, dimensions={0}, use_global_device_ids=true | all-gather | bytes 67584 | tf_op jit(solution)/shard_map/all_gather | solution.py:27
  50.9 39.2 %all_gather.18 = f32[2,8192]{1,0:T(2,128)S(1)} all-gather(f32[2,256]{1,0:T(2,128)} %param.12), channel_id=1, replica_groups=mesh['row'=8,'col'=32] {'col'}, dimensions={1}, use_global_device_ids=true | all-gather | bytes 67584 | tf_op jit(solution)/shard_map/all_gather | solution.py:26
  90.1 0.7 broadcast_compare_fusion
  90.8 23.1 %all-gather.5.cloned.1.call-done = f32[256,8192]{1,0:T(8,128)} async-done(((f32[256,256]{1,0:T(8,128)}), f32[256,8192]{1,0:T(8,128)}) %all-gather.5.cloned.1.call-update) | async-done | bytes 8388624 | tf_op jit(solution)/shard_map/all_gather | solution.py:24
  113.9 102.9 %all-gather.7.cloned.1.call-done = f32[256,8192]{1,0:T(8,128)} async-done(((f32[256,256]{1,0:T(8,128)}), f32[256,8192]{1,0:T(8,128)}) %all-gather.7.cloned.1.call-update) | async-done | bytes 8388624 | tf_op jit(solution)/shard_map/all_gather | solution.py:25
  216.8 68.3 %while.18 = (s32[]{:T(128)}, f32[256,512]{1,0:T(8,128)S(1)}, f32[256,512]{1,0:T(8,128)S(1)}, f32[512]{0:T(512)S(1)}, f32[256,8192]{1,0:T(8,128)}, /*index=5*/pre...) while((s32[]{:T(128)}, f32[256,512]{1,0:T(8,128)S(1)}, ...), condition=%wide.region_2.3_spmd.clone, body=%wide.region_0.2_spmd.clone.sunk | while | flops 3229093376 | bytes 12669679 | solution.py:48
  216.9 0.1 broadcast_add_fusion.2
  216.9 1.9 multiply_reduce_fusion.3
  218.8 3.3 %fusion.17 = f32[256,512]{1,0:T(8,128)S(1)} fusion(f32[2,1024,512]{2,1,0:T(8,128)S(1)} %get-tuple-element.347, f32[256,8192]{1,0:T(8,128)} %get-tuple-element.389, s32[]{:T(128)S(6)} %select_n.28, f32[256,512]{1,0:T(8,128)S(1)} %get-tuple-element.366, pred[]{:T(512)S(6)} %compare.3), kind=kOutput, calls=%fused_computation.9.clone.1 | convolution fusion | flops 1610874880 | bytes 4194309 | tf_op jit(solution)/shard_map/while/body/eval_jaxpr/dot_general | solution.py:43
  222.1 3.3 %fusion.16 = f32[256,512]{1,0:T(8,128)S(1)} fusion(f32[2,1024,512]{2,1,0:T(8,128)S(1)} %get-tuple-element.347, f32[256,8192]{1,0:T(8,128)} %get-tuple-element.383, s32[]{:T(128)S(6)} %select_n.28, f32[256,512]{1,0:T(8,128)S(1)} %get-tuple-element.365, pred[]{:T(512)S(6)} %compare.3), kind=kOutput, calls=%fused_computation.8.clone.1 | convolution fusion | flops 1610874880 | bytes 4194309 | tf_op jit(solution)/shard_map/while/body/eval_jaxpr/dot_general | solution.py:40
  225.4 0.1 broadcast_add_fusion.2
  225.5 1.9 multiply_reduce_fusion.3
  227.4 3.3 %fusion.17 = f32[256,512]{1,0:T(8,128)S(1)} fusion(f32[2,1024,512]{2,1,0:T(8,128)S(1)} %get-tuple-element.347, f32[256,8192]{1,0:T(8,128)} %get-tuple-element.389, s32[]{:T(128)S(6)} %select_n.28, f32[256,512]{1,0:T(8,128)S(1)} %get-tuple-element.366, pred[]{:T(512)S(6)} %compare.3), kind=kOutput, calls=%fused_computation.9.clone.1 | convolution fusion | flops 1610874880 | bytes 4194309 | tf_op jit(solution)/shard_map/while/body/eval_jaxpr/dot_general | solution.py:43
  230.6 3.3 %fusion.16 = f32[256,512]{1,0:T(8,128)S(1)} fusion(f32[2,1024,512]{2,1,0:T(8,128)S(1)} %get-tuple-element.347, f32[256,8192]{1,0:T(8,128)} %get-tuple-element.383, s32[]{:T(128)S(6)} %select_n.28, f32[256,512]{1,0:T(8,128)S(1)} %get-tuple-element.365, pred[]{:T(512)S(6)} %compare.3), kind=kOutput, calls=%fused_computation.8.clone.1 | convolution fusion | flops 1610874880 | bytes 4194309 | tf_op jit(solution)/shard_map/while/body/eval_jaxpr/dot_general | solution.py:40
  233.9 0.1 broadcast_add_fusion.2
  234.0 1.9 multiply_reduce_fusion.3
  235.9 3.3 %fusion.17 = f32[256,512]{1,0:T(8,128)S(1)} fusion(f32[2,1024,512]{2,1,0:T(8,128)S(1)} %get-tuple-element.347, f32[256,8192]{1,0:T(8,128)} %get-tuple-element.389, s32[]{:T(128)S(6)} %select_n.28, f32[256,512]{1,0:T(8,128)S(1)} %get-tuple-element.366, pred[]{:T(512)S(6)} %compare.3), kind=kOutput, calls=%fused_computation.9.clone.1 | convolution fusion | flops 1610874880 | bytes 4194309 | tf_op jit(solution)/shard_map/while/body/eval_jaxpr/dot_general | solution.py:43
  239.2 3.3 %fusion.16 = f32[256,512]{1,0:T(8,128)S(1)} fusion(f32[2,1024,512]{2,1,0:T(8,128)S(1)} %get-tuple-element.347, f32[256,8192]{1,0:T(8,128)} %get-tuple-element.383, s32[]{:T(128)S(6)} %select_n.28, f32[256,512]{1,0:T(8,128)S(1)} %get-tuple-element.365, pred[]{:T(512)S(6)} %compare.3), kind=kOutput, calls=%fused_computation.8.clone.1 | convolution fusion | flops 1610874880 | bytes 4194309 | tf_op jit(solution)/shard_map/while/body/eval_jaxpr/dot_general | solution.py:40
  242.5 0.1 broadcast_add_fusion.2
  242.6 1.9 multiply_reduce_fusion.3
  244.5 3.3 %fusion.17 = f32[256,512]{1,0:T(8,128)S(1)} fusion(f32[2,1024,512]{2,1,0:T(8,128)S(1)} %get-tuple-element.347, f32[256,8192]{1,0:T(8,128)} %get-tuple-element.389, s32[]{:T(128)S(6)} %select_n.28, f32[256,512]{1,0:T(8,128)S(1)} %get-tuple-element.366, pred[]{:T(512)S(6)} %compare.3), kind=kOutput, calls=%fused_computation.9.clone.1 | convolution fusion | flops 1610874880 | bytes 4194309 | tf_op jit(solution)/shard_map/while/body/eval_jaxpr/dot_general | solution.py:43
  247.7 3.3 %fusion.16 = f32[256,512]{1,0:T(8,128)S(1)} fusion(f32[2,1024,512]{2,1,0:T(8,128)S(1)} %get-tuple-element.347, f32[256,8192]{1,0:T(8,128)} %get-tuple-element.383, s32[]{:T(128)S(6)} %select_n.28, f32[256,512]{1,0:T(8,128)S(1)} %get-tuple-element.365, pred[]{:T(512)S(6)} %compare.3), kind=kOutput, calls=%fused_computation.8.clone.1 | convolution fusion | flops 1610874880 | bytes 4194309 | tf_op jit(solution)/shard_map/while/body/eval_jaxpr/dot_general | solution.py:40
  251.0 0.1 broadcast_add_fusion.2
  251.1 1.9 multiply_reduce_fusion.3
  253.0 3.3 %fusion.17 = f32[256,512]{1,0:T(8,128)S(1)} fusion(f32[2,1024,512]{2,1,0:T(8,128)S(1)} %get-tuple-element.347, f32[256,8192]{1,0:T(8,128)} %get-tuple-element.389, s32[]{:T(128)S(6)} %select_n.28, f32[256,512]{1,0:T(8,128)S(1)} %get-tuple-element.366, pred[]{:T(512)S(6)} %compare.3), kind=kOutput, calls=%fused_computation.9.clone.1 | convolution fusion | flops 1610874880 | bytes 4194309 | tf_op jit(solution)/shard_map/while/body/eval_jaxpr/dot_general | solution.py:43
  256.3 3.3 %fusion.16 = f32[256,512]{1,0:T(8,128)S(1)} fusion(f32[2,1024,512]{2,1,0:T(8,128)S(1)} %get-tuple-element.347, f32[256,8192]{1,0:T(8,128)} %get-tuple-element.383, s32[]{:T(128)S(6)} %select_n.28, f32[256,512]{1,0:T(8,128)S(1)} %get-tuple-element.365, pred[]{:T(512)S(6)} %compare.3), kind=kOutput, calls=%fused_computation.8.clone.1 | convolution fusion | flops 1610874880 | bytes 4194309 | tf_op jit(solution)/shard_map/while/body/eval_jaxpr/dot_general | solution.py:40
  259.6 0.1 broadcast_add_fusion.2
  259.6 1.9 multiply_reduce_fusion.3
  261.5 3.3 %fusion.17 = f32[256,512]{1,0:T(8,128)S(1)} fusion(f32[2,1024,512]{2,1,0:T(8,128)S(1)} %get-tuple-element.347, f32[256,8192]{1,0:T(8,128)} %get-tuple-element.389, s32[]{:T(128)S(6)} %select_n.28, f32[256,512]{1,0:T(8,128)S(1)} %get-tuple-element.366, pred[]{:T(512)S(6)} %compare.3), kind=kOutput, calls=%fused_computation.9.clone.1 | convolution fusion | flops 1610874880 | bytes 4194309 | tf_op jit(solution)/shard_map/while/body/eval_jaxpr/dot_general | solution.py:43
  264.8 3.3 %fusion.16 = f32[256,512]{1,0:T(8,128)S(1)} fusion(f32[2,1024,512]{2,1,0:T(8,128)S(1)} %get-tuple-element.347, f32[256,8192]{1,0:T(8,128)} %get-tuple-element.383, s32[]{:T(128)S(6)} %select_n.28, f32[256,512]{1,0:T(8,128)S(1)} %get-tuple-element.365, pred[]{:T(512)S(6)} %compare.3), kind=kOutput, calls=%fused_computation.8.clone.1 | convolution fusion | flops 1610874880 | bytes 4194309 | tf_op jit(solution)/shard_map/while/body/eval_jaxpr/dot_general | solution.py:40
  268.1 0.1 broadcast_add_fusion.2
  268.2 1.9 multiply_reduce_fusion.3
  270.1 3.3 %fusion.17 = f32[256,512]{1,0:T(8,128)S(1)} fusion(f32[2,1024,512]{2,1,0:T(8,128)S(1)} %get-tuple-element.347, f32[256,8192]{1,0:T(8,128)} %get-tuple-element.389, s32[]{:T(128)S(6)} %select_n.28, f32[256,512]{1,0:T(8,128)S(1)} %get-tuple-element.366, pred[]{:T(512)S(6)} %compare.3), kind=kOutput, calls=%fused_computation.9.clone.1 | convolution fusion | flops 1610874880 | bytes 4194309 | tf_op jit(solution)/shard_map/while/body/eval_jaxpr/dot_general | solution.py:43
  273.3 3.3 %fusion.16 = f32[256,512]{1,0:T(8,128)S(1)} fusion(f32[2,1024,512]{2,1,0:T(8,128)S(1)} %get-tuple-element.347, f32[256,8192]{1,0:T(8,128)} %get-tuple-element.383, s32[]{:T(128)S(6)} %select_n.28, f32[256,512]{1,0:T(8,128)S(1)} %get-tuple-element.365, pred[]{:T(512)S(6)} %compare.3), kind=kOutput, calls=%fused_computation.8.clone.1 | convolution fusion | flops 1610874880 | bytes 4194309 | tf_op jit(solution)/shard_map/while/body/eval_jaxpr/dot_general | solution.py:40
  276.6 0.1 broadcast_add_fusion.2
  276.7 1.9 multiply_reduce_fusion.3
  278.6 3.3 %fusion.17 = f32[256,512]{1,0:T(8,128)S(1)} fusion(f32[2,1024,512]{2,1,0:T(8,128)S(1)} %get-tuple-element.347, f32[256,8192]{1,0:T(8,128)} %get-tuple-element.389, s32[]{:T(128)S(6)} %select_n.28, f32[256,512]{1,0:T(8,128)S(1)} %get-tuple-element.366, pred[]{:T(512)S(6)} %compare.3), kind=kOutput, calls=%fused_computation.9.clone.1 | convolution fusion | flops 1610874880 | bytes 4194309 | tf_op jit(solution)/shard_map/while/body/eval_jaxpr/dot_general | solution.py:43
  281.9 3.3 %fusion.16 = f32[256,512]{1,0:T(8,128)S(1)} fusion(f32[2,1024,512]{2,1,0:T(8,128)S(1)} %get-tuple-element.347, f32[256,8192]{1,0:T(8,128)} %get-tuple-element.383, s32[]{:T(128)S(6)} %select_n.28, f32[256,512]{1,0:T(8,128)S(1)} %get-tuple-element.365, pred[]{:T(512)S(6)} %compare.3), kind=kOutput, calls=%fused_computation.8.clone.1 | convolution fusion | flops 1610874880 | bytes 4194309 | tf_op jit(solution)/shard_map/while/body/eval_jaxpr/dot_general | solution.py:40
  285.2 0.7 rsqrt_select_fusion
  285.8 0.1 multiply_bitcast_fusion.1
  286.0 1.1 multiply_reduce_fusion.1
  287.1 15.6 %psum.7 = f32[512]{0:T(512)S(1)} all-reduce(f32[512]{0:T(512)S(1)} %get-tuple-element.266), channel_id=1, replica_groups=mesh['row'=8,'col'=32] {'row'}, use_global_device_ids=true, to_apply=%region_4.5 | all-reduce | flops 512 | bytes 4096 | tf_op jit(solution)/shard_map/psum | solution.py:57
  302.7 0.6 broadcast_multiply_fusion
  (35 shorter events, 0.2 us)
Async XLA Ops:
  7.2 106.8 %all-gather.5.cloned.1.call-start = ((), (), s32[]{:S(2)}) async-start(), calls=%async_computation | async-start | bytes 8650752 | tf_op jit(solution)/shard_map/all_gather | solution.py:24
  7.9 209.0 %all-gather.7.cloned.1.call-start = ((), (), s32[]{:S(2)}) async-start(), calls=%async_computation.1 | async-start | bytes 8650752 | tf_op jit(solution)/shard_map/all_gather | solution.py:25
Sparse Core Ops, SparseCore 0:
  10.4 103.4 all-gather.4
  116.4 100.4 all-gather.6
